TPU v7x, 32 devices: a whole 2x2x4 slice. The times are simulated.
32 devices in a mesh: row: 4 (over y, core), col: 8 (over z, x).
Axes of the slice: x: 2, y: 2, z: 4, core: 2. Of those that a mesh axis runs over, the one named last changes fastest.
Arguments:
- matrix: float32 [32768, 1024], P('row', 'col'), may hold values from -700 to 700, as said below
Outputs:
- r_rows: float32 [2, 128, 1024], P(None, None, 'col')
- factored: float32 [32768, 1024], P('row', 'col')
Inputs may be any that keep to these rules, and one draw needn't show every extreme that they name: `matrix`: real-valued entries.
All inputs are finite; a program needn't handle non-finite values.
Results may differ from a plain program's by a relative error of at most 0.0003.
Values sent between devices are 32-bit elements; how exact they have to be, the bound alone decides.
A program may use at most 64 MiB of HBM per device.

v0:
```python
import math

import jax
import jax.numpy as jnp
from jax import lax
from jax.sharding import PartitionSpec as P


def broadcast(block, axis, holder):
    block = jnp.where(lax.axis_index(axis) == holder, block, jnp.zeros_like(block))
    return lax.psum(block, axis)


def gram_matrix(block):
    return lax.dot_general(block, block, (((0,), (0,)), ((), ())), precision=lax.Precision.HIGHEST)


def inverse_of(lower_factor):
    width = lower_factor.shape[0]
    return jax.scipy.linalg.solve_triangular(
        lower_factor, jnp.eye(width, dtype=jnp.float32), lower=True
    )


def local(matrix):
    rows_total = matrix.shape[0] * lax.axis_size("row")
    factor_scale = math.sqrt(rows_total)
    col_index = lax.axis_index("col")
    current = matrix
    couplings = []
    stored = []
    for panel_id in range(2):
        panel_rows = broadcast(current, "col", panel_id)
        local_gram = gram_matrix(panel_rows)
        local_mixed = lax.dot_general(
            panel_rows, current, (((0,), (0,)), ((), ())), precision=lax.Precision.HIGHEST
        )
        gram_sums, mixed_sums = lax.psum((local_gram, local_mixed), "row")
        lower_factor = jnp.linalg.cholesky(gram_sums)
        inverse_lower = inverse_of(lower_factor)
        basis_rows = lax.dot_general(
            panel_rows, inverse_lower, (((1,), (1,)), ((), ())), precision=lax.Precision.HIGHEST
        )
        cross_rows = jnp.dot(inverse_lower, mixed_sums, precision=lax.Precision.HIGHEST)
        updated = current - jnp.dot(basis_rows, cross_rows, precision=lax.Precision.HIGHEST)
        scaled_basis = factor_scale * basis_rows
        current = jnp.where(col_index == panel_id, scaled_basis, updated)
        stored.append(scaled_basis)
        couplings.append(cross_rows / factor_scale)
    factored = jnp.where(col_index == 0, stored[0], current)
    return (jnp.stack(couplings), factored)


def solution(mesh):
    return jax.shard_map(
        local,
        mesh=mesh,
        in_specs=(P("row", "col"),),
        out_specs=(P(None, None, "col"), P("row", "col")),
        check_vma=False,
    )
```

profile of v0, /device:TPU:0, one launch (start us, length us, event | category | flops | bytes accessed | tf_op | source)
XLA Modules:
  0.0 509.6 jit_solution(12433639063543856480)
XLA Ops:
  7.2 0.0 all-reduce.7.cloned.1.call-start
  7.2 4.5 broadcast_select_fusion.1
  11.7 0.0 all-reduce.7.cloned.1.call-update
  11.7 0.0 all-reduce.13.cloned.1.call-start
  11.8 159.6 %all-reduce.7.cloned.1.call-done = f32[8192,128]{1,0:T(8,128)} async-done(((f32[8192,128]{1,0:T(8,128)}), f32[8192,128]{1,0:T(8,128)}) %all-reduce.7.cloned.1.call-update) | async-done | bytes 4194320 | tf_op jit(solution)/shard_map/psum | solution.py:11
  171.4 11.0 %fusion.14 = f32[128,128]{1,0:T(8,128)} fusion(f32[8192,128]{1,0:T(8,128)} %all-reduce.7.cloned.1.call-done, f32[8192,128]{1,0:T(8,128)} %param.4), kind=kOutput, calls=%fused_computation.31 | convolution fusion | flops 1610612736 | bytes 8454144 | tf_op jit(solution)/shard_map/dot_general | solution.py:35
  182.3 0.0 copy-done
  182.3 7.7 %fusion.13 = f32[128,128]{0,1:T(8,128)} fusion(f32[8192,128]{1,0:T(8,128)S(1)} %copy-done), kind=kOutput, calls=%fused_computation.30 | convolution fusion | flops 1610612736 | bytes 4259840 | tf_op jit(solution)/shard_map/dot_general | solution.py:15
  190.0 0.0 all-reduce.13.cloned.1.call-update
  190.0 0.0 all-reduce.9.cloned.1.call-start
  190.1 30.9 %all-reduce.13.cloned.1.call-done = (f32[128,128]{0,1:T(8,128)}, f32[128,128]{1,0:T(8,128)}) async-done(((f32[128,128]{0,1:T(8,128)}, f32[128,128]{1,0:T(8,128)}), (f32[128,128]{0,1:T(8,128)}, f32[128,128]{1,0:T(8,128)})) %all-reduce.13.cloned.1.call-update) | async-done | bytes 131088 | tf_op jit(solution)/shard_map/psum | solution.py:38
  221.0 0.9 copy.4
  222.0 0.9 fusion.12
  222.8 11.7 %cholesky.44 = f32[128,128]{1,0:T(8,128)S(1)} custom-call(f32[128,128]{1,0:T(8,128)S(1)} %fusion.12), custom_call_target="Cholesky" | custom-call | tf_op jit(solution)/shard_map/jit(cholesky)/cholesky | solution.py:39
  234.6 0.6 compare_reduce_fusion.1
  235.2 0.7 fusion.7
  235.9 9.8 %custom-call.6 = f32[1,128,128]{1,2,0:T(8,128)S(1)} custom-call(f32[1,128,128]{2,1,0:T(8,128)S(1)} %fusion.7), custom_call_target="InvertDiagBlocksLowerTriangular" | custom-call | tf_op jit(solution)/shard_map/jit(_solve_triangular)/triangular_solve | solution.py:20
  245.7 0.3 fusion.5
  246.0 1.0 fusion.15
  247.0 0.0 copy-start.4
  247.0 5.5 %fusion.16 = f32[8192,128]{1,0:T(8,128)S(1)} fusion(f32[8192,128]{1,0:T(8,128)} %all-reduce.7.cloned.1.call-done, f32[128,128]{1,0:T(8,128)S(1)} %fusion.5), kind=kOutput, calls=%fused_computation.33 | convolution fusion | flops 1610612736 | bytes 8454144 | tf_op jit(solution)/shard_map/dot_general | solution.py:41
  252.5 0.0 copy-done.4
  252.6 0.0 copy-start.2
  252.6 5.8 %broadcast_select_fusion = (f32[8192,128]{1,0:T(8,128)}, f32[8192,128]{1,0:T(8,128)}) fusion(pred[]{:T(512)S(6)} %eq.17, f32[8192,128]{1,0:T(8,128)S(1)} %copy-done.4, f32[8192,128]{1,0:T(8,128)S(1)} %fusion.16, f32[128,128]{1,0:T(8,128)S(1)} %fusion.15, pred[]{:T(512)S(6)} %eq.15), kind=kOutput, calls=%fused_computation.5 | convolution fusion | flops 1614807040 | bytes 16842754 | tf_op jit(solution)/shard_map/dot_general | solution.py:45
  258.4 0.0 copy-done.2
  258.4 0.0 all-reduce.9.cloned.1.call-update
  258.4 0.2 all-reduce.11.cloned.1.call-start
  258.7 156.3 %all-reduce.9.cloned.1.call-done = f32[8192,128]{1,0:T(8,128)} async-done(((f32[8192,128]{1,0:T(8,128)}), f32[8192,128]{1,0:T(8,128)}) %all-reduce.9.cloned.1.call-update) | async-done | bytes 4194320 | tf_op jit(solution)/shard_map/psum | solution.py:11
  415.0 11.0 %fusion.17 = f32[128,128]{0,1:T(8,128)} fusion(f32[8192,128]{1,0:T(8,128)} %all-reduce.9.cloned.1.call-done), kind=kOutput, calls=%fused_computation.34 | convolution fusion | flops 1610612736 | bytes 4259840 | tf_op jit(solution)/shard_map/dot_general | solution.py:15
  426.0 0.0 copy-done.1
  426.0 0.0 copy-done.5
  426.0 7.6 %fusion.18 = f32[128,128]{1,0:T(8,128)} fusion(f32[8192,128]{1,0:T(8,128)S(1)} %copy-done.1, f32[8192,128]{1,0:T(8,128)S(1)} %copy-done.5), kind=kOutput, calls=%fused_computation.35 | convolution fusion | flops 1610612736 | bytes 8454144 | tf_op jit(solution)/shard_map/dot_general | solution.py:35
  433.5 0.0 all-reduce.11.cloned.1.call-update
  433.6 31.0 %all-reduce.11.cloned.1.call-done = (f32[128,128]{0,1:T(8,128)}, f32[128,128]{1,0:T(8,128)}) async-done(((f32[128,128]{0,1:T(8,128)}, f32[128,128]{1,0:T(8,128)}), (f32[128,128]{0,1:T(8,128)}, f32[128,128]{1,0:T(8,128)})) %all-reduce.11.cloned.1.call-update) | async-done | bytes 131088 | tf_op jit(solution)/shard_map/psum | solution.py:38
  464.6 0.9 copy.6
  465.5 0.9 fusion.10
  466.4 11.7 %cholesky.55 = f32[128,128]{1,0:T(8,128)S(1)} custom-call(f32[128,128]{1,0:T(8,128)S(1)} %fusion.10), custom_call_target="Cholesky" | custom-call | tf_op jit(solution)/shard_map/jit(cholesky)/cholesky | solution.py:39
  478.1 0.6 compare_reduce_fusion
  478.7 0.7 fusion.8
  479.4 9.8 %custom-call.7 = f32[1,128,128]{1,2,0:T(8,128)S(1)} custom-call(f32[1,128,128]{2,1,0:T(8,128)S(1)} %fusion.8), custom_call_target="InvertDiagBlocksLowerTriangular" | custom-call | tf_op jit(solution)/shard_map/jit(_solve_triangular)/triangular_solve | solution.py:20
  489.2 0.3 fusion.3
  489.5 1.0 fusion.19
  490.6 0.0 copy-start.3
  490.6 0.0 copy-start.6
  490.6 5.7 %fusion.20 = f32[8192,128]{1,0:T(8,128)S(1)} fusion(f32[8192,128]{1,0:T(8,128)} %all-reduce.9.cloned.1.call-done, f32[128,128]{1,0:T(8,128)S(1)} %fusion.3), kind=kOutput, calls=%fused_computation.37 | convolution fusion | flops 1610612736 | bytes 8454144 | tf_op jit(solution)/shard_map/dot_general | solution.py:41
  496.4 0.0 copy-done.3
  496.4 5.6 %fusion.2 = f32[8192,128]{1,0:T(8,128)} fusion(f32[8192,128]{1,0:T(8,128)S(1)} %copy-done.6, f32[8192,128]{1,0:T(8,128)S(1)} %fusion.20, f32[128,128]{1,0:T(8,128)S(1)} %fusion.19, f32[8192,128]{1,0:T(8,128)S(1)} %copy-done.3, pred[]{:T(512)S(6)} %eq.17, pred[]{:T(512)S(6)} %eq.15), kind=kOutput, calls=%fused_computation.4 | convolution fusion | flops 1615855616 | bytes 16842754 | tf_op jit(solution)/shard_map/dot_general | solution.py:45
  502.0 0.7 pad_maximum_fusion
  (8 shorter events, 0.1 us)
Async XLA Ops:
  7.2 164.2 %all-reduce.7.cloned.1.call-start = ((), (), s32[]{:S(2)}) async-start(), calls=%async_computation | async-start | bytes 8388608 | tf_op jit(solution)/shard_map/psum | solution.py:11
  11.7 209.3 %all-reduce.13.cloned.1.call-start = ((), (), s32[]{:S(2)}) async-start(), calls=%async_computation.3 | async-start | bytes 262144 | tf_op jit(solution)/shard_map/psum | solution.py:38
  171.4 11.0 %copy-start = (f32[8192,128]{1,0:T(8,128)S(1)}, f32[8192,128]{1,0:T(8,128)}, u32[]{:S(2)}) copy-start(f32[8192,128]{1,0:T(8,128)} %all-reduce.7.cloned.1.call-done) | copy-start | bytes 12582916
  190.0 225.0 %all-reduce.9.cloned.1.call-start = ((), (), s32[]{:S(2)}) async-start(), calls=%async_computation.1 | async-start | bytes 8388608 | tf_op jit(solution)/shard_map/psum | solution.py:11
  247.0 5.5 %copy-start.4 = (f32[8192,128]{1,0:T(8,128)S(1)}, f32[8192,128]{1,0:T(8,128)}, u32[]{:S(2)}) copy-start(f32[8192,128]{1,0:T(8,128)} %param.4) | copy-start | bytes 12582916
  252.6 5.9 %copy-start.2 = (f32[8192,128]{1,0:T(8,128)}, f32[8192,128]{1,0:T(8,128)S(1)}, u32[]{:S(2)}) copy-start(f32[8192,128]{1,0:T(8,128)S(1)} %fusion.16) | copy-start | bytes 12582916
  258.4 206.1 %all-reduce.11.cloned.1.call-start = ((), (), s32[]{:S(2)}) async-start(), calls=%async_computation.2 | async-start | bytes 262144 | tf_op jit(solution)/shard_map/psum | solution.py:38
  415.0 11.0 %copy-start.1 = (f32[8192,128]{1,0:T(8,128)S(1)}, f32[8192,128]{1,0:T(8,128)}, u32[]{:S(2)}) copy-start(f32[8192,128]{1,0:T(8,128)} %all-reduce.9.cloned.1.call-done) | copy-start | bytes 12582916
  415.0 11.0 %copy-start.5 = (f32[8192,128]{1,0:T(8,128)S(1)}, f32[8192,128]{1,0:T(8,128)}, u32[]{:S(2)}) copy-start(f32[8192,128]{1,0:T(8,128)} %get-tuple-element.9) | copy-start | bytes 12582916
  490.6 5.8 %copy-start.3 = (f32[8192,128]{1,0:T(8,128)S(1)}, f32[8192,128]{1,0:T(8,128)}, u32[]{:S(2)}) copy-start(f32[8192,128]{1,0:T(8,128)} %copy-done.2) | copy-start | bytes 12582916
  490.6 5.8 %copy-start.6 = (f32[8192,128]{1,0:T(8,128)S(1)}, f32[8192,128]{1,0:T(8,128)}, u32[]{:S(2)}) copy-start(f32[8192,128]{1,0:T(8,128)} %get-tuple-element.9) | copy-start | bytes 12582916
Sparse Core Ops, SparseCore 0:
  12.2 159.0 all-reduce.6
  190.2 30.8 all-reduce.12
  258.6 156.3 all-reduce.8
  433.7 30.8 all-reduce.10
where the time goes:
time: 519 us; the launch traced here: 510 us
  waiting for transfers between devices  378 us (73%)
  matrix products  62.5 us (12%)
  other arithmetic  52.6 us (10%)
  between operations  14.4 us (3%)
    psum x2, waiting for transfers between devices, broadcast(): return lax.psum(block, axis)  316 us
    psum x2, waiting for transfers between devices, local(): gram_sums, mixed_sums = lax.psum((local_gram, local_mixed), 'row')  61.9 us
    another operation x6, other arithmetic, local(): lower_factor = jnp.linalg.cholesky(gram_sums)  24.8 us
    another operation x4, other arithmetic, inverse_of(): jax.scipy.linalg.solve_triangular(lower_factor, jnp.eye(width, dtype=jnp....  20.9 us
    dot_general x2, matrix products, gram_matrix(): lax.dot_general(block, block, (((0,), (0,)), ((), ())), precision=lax.Pre...  18.7 us
    dot_general x2, matrix products, local(): lax.dot_general(panel_rows, current, (((0,), (0,)), ((), ())), precision=...  18.5 us
    dot_general x2, matrix products, local(): jnp.dot(basis_rows, cross_rows, precision=lax.Precision.HIGHEST)  11.4 us
    dot_general x2, matrix products, local(): lax.dot_general(panel_rows, inverse_lower, (((1,), (1,)), ((), ())), prec...  11.2 us
  transfers between devices with their start and end apart: 4, of which 4 were waited for; matrix products, arithmetic and copies ran while one was open for 0% of the time, Pallas kernels for 0%

commit v1 on v0

v1 whole, which is shorter than its diff:
```python
import functools
import math

import jax
import jax.numpy as jnp
from jax import lax
from jax.experimental import pallas as pl
from jax.experimental.pallas import tpu as pltpu
from jax.sharding import PartitionSpec as P

MESH = pl.DeviceIdType.MESH
HIGHEST = lax.Precision.HIGHEST
PANELS = 2
LAG = 3


def outer(a, b):
    return lax.dot_general(
        a, b, (((0,), (0,)), ((), ())), precision=HIGHEST, preferred_element_type=jnp.float32
    )


def gather_kernel(
    n_row, n_x, n_z, tile,
    matrix_ref, panels_out, sums_out,
    panels, mine, sums, parts, total,
    mine_sem, recv_sem, send_sem, out_sem, rs_send, rs_recv, ag_send, ag_recv,
):
    rows, width = mine.shape
    steps = rows // tile
    row = lax.axis_index("row")
    col = lax.axis_index("col")
    x = lax.rem(col, n_x)
    z = col // n_x

    barrier = pltpu.get_barrier_semaphore()
    neighbours = (
        (x > 0, col - 1), (x < n_x - 1, col + 1), (z > 0, col - n_x), (z < n_z - 1, col + n_x)
    )
    for there, other in neighbours:
        @pl.when(there)
        def _():
            pl.semaphore_signal(barrier, inc=1, device_id={"col": other}, device_id_type=MESH)
    for step in range(1, n_row):
        peer = lax.rem(row + step, n_row)
        pl.semaphore_signal(barrier, inc=1, device_id={"row": peer}, device_id_type=MESH)
    load_mine = pltpu.make_async_copy(matrix_ref, mine, mine_sem)
    load_mine.start()
    peers = n_row - 1
    for there, _ in neighbours:
        peers += jnp.where(there, 1, 0)
    pl.semaphore_wait(barrier, peers)

    def span(index):
        return pl.ds(pl.multiple_of(index * tile, tile), tile)

    def children(panel):
        return (
            (jnp.logical_and(x == panel, z < n_z - 1), col + n_x),
            (jnp.logical_and(x >= panel, x < n_x - 1), col + 1),
            (jnp.logical_and(x <= panel, x > 0), col - 1),
        )

    def forward(panel, index, source):
        for child, (there, other) in enumerate(children(panel)):
            @pl.when(there)
            def _():
                pltpu.make_async_remote_copy(
                    src_ref=source.at[span(index)],
                    dst_ref=panels.at[panel, span(index)],
                    send_sem=send_sem.at[panel, child],
                    recv_sem=recv_sem.at[panel, index],
                    device_id={"col": other},
                    device_id_type=MESH,
                ).start()

    owner = col < PANELS

    @pl.when(owner)
    def _():
        @pl.loop(0, steps)
        def _(index):
            forward(col, index, matrix_ref)
            pltpu.make_async_copy(
                matrix_ref.at[span(index)], panels.at[col, span(index)], recv_sem.at[col, index]
            ).start()

    main = jnp.where(x == 1, 1, 0)
    second = 1 - main

    def take(panel, index):
        pltpu.make_async_copy(
            matrix_ref.at[span(index)], panels.at[panel, span(index)], recv_sem.at[panel, index]
        ).wait()

        @pl.when(col != panel)
        def _():
            forward(panel, index, panels.at[panel])

        pltpu.make_async_copy(
            panels.at[panel, span(index)], panels_out.at[panel, span(index)], out_sem.at[panel]
        ).start()

    sums[...] = jnp.zeros_like(sums)
    load_mine.wait()

    @pl.loop(0, steps + LAG)
    def _(step):
        @pl.when(step < steps)
        def _():
            take(main, step)

        @pl.when(step >= LAG)
        def _():
            index = step - LAG
            take(second, index)
            first = panels[0, span(index)]
            other = panels[1, span(index)]
            both = jnp.concatenate([first, other], axis=1)
            right = jnp.concatenate([first, other, mine[span(index)]], axis=1)
            sums[...] += outer(both, right)

    share = sums.shape[0] // n_row

    def part(index):
        return pl.ds(pl.multiple_of(index * share, share), share)

    scatters = []
    for step in range(1, n_row):
        peer = lax.rem(row + step, n_row)
        copy = pltpu.make_async_remote_copy(
            src_ref=sums.at[part(peer)],
            dst_ref=parts.at[step - 1],
            send_sem=rs_send.at[step - 1],
            recv_sem=rs_recv.at[step - 1],
            device_id={"row": peer},
            device_id_type=MESH,
        )
        copy.start()
        scatters.append(copy)
    summed = sums[part(row)]
    for step, copy in enumerate(scatters):
        copy.wait_recv()
        summed += parts[step]
    total[part(row)] = summed
    gathers = []
    for step in range(1, n_row):
        peer = lax.rem(row + step, n_row)
        copy = pltpu.make_async_remote_copy(
            src_ref=total.at[part(row)],
            dst_ref=total.at[part(row)],
            send_sem=ag_send.at[step - 1],
            recv_sem=ag_recv.at[step - 1],
            device_id={"row": peer},
            device_id_type=MESH,
        )
        copy.start()
        gathers.append(copy)
    for copy in gathers:
        copy.wait_recv()
    sums_out[...] = total[...]

    for copy in scatters + gathers:
        copy.wait_send()
    for panel in range(PANELS):
        pltpu.make_async_copy(panels.at[panel], panels_out.at[panel], out_sem.at[panel]).wait()
        for child, (there, other) in enumerate(children(panel)):
            @pl.when(there)
            def _():
                pltpu.make_async_remote_copy(
                    src_ref=panels.at[panel],
                    dst_ref=panels.at[panel],
                    send_sem=send_sem.at[panel, child],
                    recv_sem=recv_sem.at[panel, 0],
                    device_id={"col": other},
                    device_id_type=MESH,
                ).wait_send()


def gather(matrix, n_row, n_x, n_z):
    rows, width = matrix.shape
    tile = math.gcd(rows, 256)
    steps = rows // tile
    deep, wide = PANELS * width, (PANELS + 1) * width
    share = deep // n_row
    anywhere = pl.BlockSpec(memory_space=pl.ANY)
    return pl.pallas_call(
        functools.partial(gather_kernel, n_row, n_x, n_z, tile),
        out_shape=(
            jax.ShapeDtypeStruct((PANELS, rows, width), jnp.float32),
            jax.ShapeDtypeStruct((deep, wide), jnp.float32),
        ),
        in_specs=[anywhere],
        out_specs=(anywhere, pl.BlockSpec(memory_space=pltpu.VMEM)),
        scratch_shapes=[
            pltpu.VMEM((PANELS, rows, width), jnp.float32),
            pltpu.VMEM((rows, width), jnp.float32),
            pltpu.VMEM((deep, wide), jnp.float32),
            pltpu.VMEM((n_row - 1, share, wide), jnp.float32),
            pltpu.VMEM((deep, wide), jnp.float32),
            pltpu.SemaphoreType.DMA,
            pltpu.SemaphoreType.DMA((PANELS, steps)),
            pltpu.SemaphoreType.DMA((PANELS, 3)),
            pltpu.SemaphoreType.DMA((PANELS,)),
            pltpu.SemaphoreType.DMA((n_row - 1,)),
            pltpu.SemaphoreType.DMA((n_row - 1,)),
            pltpu.SemaphoreType.DMA((n_row - 1,)),
            pltpu.SemaphoreType.DMA((n_row - 1,)),
        ],
        compiler_params=pltpu.CompilerParams(
            collective_id=0, has_side_effects=True, vmem_limit_bytes=60 * 1024 * 1024
        ),
    )(matrix)


def update_kernel(panels_ref, matrix_ref, mix_ref, out_ref):
    width = matrix_ref.shape[1]
    keep = lax.axis_index("col") >= PANELS
    product = jnp.dot(panels_ref[0], mix_ref[:width], precision=HIGHEST)
    product += jnp.dot(panels_ref[1], mix_ref[width:], precision=HIGHEST)
    out_ref[...] = jnp.where(keep, matrix_ref[...], 0.0) - product


def update(panels, matrix, mix):
    rows, width = matrix.shape
    tile = math.gcd(rows, 1024)
    return pl.pallas_call(
        update_kernel,
        grid=(rows // tile,),
        out_shape=jax.ShapeDtypeStruct((rows, width), jnp.float32),
        in_specs=[
            pl.BlockSpec((PANELS, tile, width), lambda i: (0, i, 0)),
            pl.BlockSpec((tile, width), lambda i: (i, 0)),
            pl.BlockSpec((PANELS * width, width), lambda i: (0, 0)),
        ],
        out_specs=pl.BlockSpec((tile, width), lambda i: (i, 0)),
        compiler_params=pltpu.CompilerParams(vmem_limit_bytes=40 * 1024 * 1024),
    )(panels, matrix, mix)


def product(a, b):
    return jnp.dot(a, b, precision=HIGHEST)


def inverse_of(lower_factor):
    width = lower_factor.shape[0]
    return jax.scipy.linalg.solve_triangular(
        lower_factor, jnp.eye(width, dtype=jnp.float32), lower=True
    )


def coefficients(sums, factor_scale, width):
    col = lax.axis_index("col")
    g00, g01 = sums[:width, :width], sums[:width, width:2 * width]
    g11 = sums[width:, width:2 * width]
    m0, m1 = sums[:width, 2 * width:], sums[width:, 2 * width:]
    scaled_eye = factor_scale * jnp.eye(width, dtype=jnp.float32)
    inv0 = inverse_of(jnp.linalg.cholesky(g00))
    both = product(inv0, jnp.concatenate([m0, g01], axis=1))
    cross0, r01 = both[:, :width], both[:, width:]
    lower1 = jnp.linalg.cholesky(g11 - product(r01.T, r01))
    inv1 = inverse_of(lower1)
    scaled = factor_scale * product(jnp.concatenate([g00, g01.T], axis=0), inv0.T)
    n0 = jnp.where(col == 0, scaled[:width], m0)
    n1 = jnp.where(col == 0, scaled[width:], m1)
    cross1 = product(inv1, n1 - product(r01.T, product(inv0, n0)))
    t1 = jnp.where(col == 1, -scaled_eye, jnp.where(col == 0, 0.0, cross1))
    t0 = jnp.where(col == 0, -scaled_eye, jnp.where(col == 1, 0.0, cross0))
    x1 = product(inv1.T, t1)
    x0 = product(inv0.T, t0 - product(r01, x1))
    return jnp.stack([cross0, cross1]) / factor_scale, jnp.concatenate([x0, x1], axis=0)


def solution(mesh):
    n_row, n_col = mesh.shape["row"], mesh.shape["col"]
    n_x = max(PANELS, n_row // 2)
    n_z = n_col // n_x
    assert n_x * n_z == n_col

    def local(matrix):
        rows, width = matrix.shape
        factor_scale = math.sqrt(rows * n_row)
        panels, sums = gather(matrix, n_row, n_x, n_z)
        r_rows, mix = coefficients(sums, factor_scale, width)
        return r_rows, update(panels, matrix, mix)

    return jax.shard_map(
        local,
        mesh=mesh,
        in_specs=(P("row", "col"),),
        out_specs=(P(None, None, "col"), P("row", "col")),
        check_vma=False,
    )
```

time: 519 us -> 189 us (0.36)
  the two profiles are of different devices: /device:TPU:0 before, /device:TPU:25 now
where the time goes in v1:
time: 189 us
  Pallas kernels  129 us (68%)
  other arithmetic  46.5 us (25%)
  local copies, waits for them, and re-layouts  7.8 us (4%)
  matrix products  4.66 us (2%)
    pallas_call x1, Pallas kernels, gather(): pl.pallas_call(functools.partial(gather_kernel, n_row, n_x, n_z, tile), o...  119 us
    another operation x4, other arithmetic, inverse_of(): jax.scipy.linalg.solve_triangular(lower_factor, jnp.eye(width, dtype=jnp....  21 us
    another operation x3, other arithmetic, coefficients(): inv0 = inverse_of(jnp.linalg.cholesky(g00))  12.4 us
    another operation x3, other arithmetic, coefficients(): lower1 = jnp.linalg.cholesky(g11 - product(r01.T, r01))  12.4 us
    pallas_call x1, Pallas kernels, update(): pl.pallas_call(update_kernel, grid=(rows // tile,), out_shape=jax.ShapeDt...  9.55 us
    unnamed x4, local copies, waits for them, and re-layouts  5.56 us
    dot_general x9, matrix products, product(): return jnp.dot(a, b, precision=HIGHEST)  4.09 us

profile of v1, /device:TPU:25, one launch (start us, length us, event | category | flops | bytes accessed | tf_op | source)
XLA Modules:
  0.0 188.6 jit_solution(11474680946521152540)
XLA Ops:
  0.6 119.2 %shard_map.30 = (f32[2,8192,128]{2,1,0:T(8,128)}, f32[256,384]{1,0:T(8,128)}) custom-call(f32[8192,128]{1,0:T(8,128)} %matrix_ref.3), custom_call_target="tpu_custom_call" | custom-call | tf_op jit(solution)/shard_map/pallas_call | solution.py:187
  119.8 0.9 slice_bitcast_fusion.1
  120.7 1.2 copy.3
  121.9 0.1 copy.4
  122.0 11.7 %cholesky.44 = f32[128,128]{1,0:T(8,128)S(1)} custom-call(f32[128,128]{1,0:T(8,128)S(1)} %fusion.17), custom_call_target="Cholesky" | custom-call | tf_op jit(solution)/shard_map/jit(cholesky)/cholesky | solution.py:258
  133.8 0.6 compare_reduce_fusion.1
  134.4 0.7 fusion.11
  135.1 9.8 %custom-call.6 = f32[1,128,128]{1,2,0:T(8,128)S(1)} custom-call(f32[1,128,128]{2,1,0:T(8,128)S(1)} %fusion.11), custom_call_target="InvertDiagBlocksLowerTriangular" | custom-call | tf_op jit(solution)/shard_map/jit(_solve_triangular)/triangular_solve | solution.py:247
  144.9 0.3 fusion.9
  145.2 0.3 fusion
  145.5 0.3 convolution_subtract_fusion.2
  145.8 0.4 convolution_multiply_fusion
  146.2 1.0 fusion.13
  147.2 1.1 convolution_subtract_fusion.1
  148.3 0.1 copy.7
  148.5 11.7 %cholesky.55 = f32[128,128]{1,0:T(8,128)S(1)} custom-call(f32[128,128]{1,0:T(8,128)S(1)} %fusion.15), custom_call_target="Cholesky" | custom-call | tf_op jit(solution)/shard_map/jit(cholesky)/cholesky | solution.py:261
  160.2 0.6 compare_reduce_fusion
  160.8 0.7 fusion.12
  161.5 9.9 %custom-call.7 = f32[1,128,128]{1,2,0:T(8,128)S(1)} custom-call(f32[1,128,128]{2,1,0:T(8,128)S(1)} %fusion.12), custom_call_target="InvertDiagBlocksLowerTriangular" | custom-call | tf_op jit(solution)/shard_map/jit(_solve_triangular)/triangular_solve | solution.py:247
  171.4 0.3 fusion.7
  171.7 0.2 fusion.38
  171.9 0.3 fusion.22
  172.2 0.2 convolution_subtract_fusion
  172.5 0.3 fusion.39
  172.8 0.0 copy-start
  172.8 2.2 %copy-done = f32[8192,128]{1,0:T(8,128)S(1)} copy-done((f32[8192,128]{1,0:T(8,128)S(1)}, f32[8192,128]{1,0:T(8,128)}, u32[]{:S(2)}) %copy-start) | copy-done | bytes 4194328
  175.0 0.0 copy-start.1
  175.0 3.4 %copy-done.1 = f32[2,8192,128]{2,1,0:T(8,128)S(1)} copy-done((f32[2,8192,128]{2,1,0:T(8,128)S(1)}, f32[2,8192,128]{2,1,0:T(8,128)}, u32[]{:S(2)}) %copy-start.1) | copy-done | bytes 8388632
  178.4 9.6 %shard_map.31 = f32[8192,128]{1,0:T(8,128)} custom-call(f32[2,8192,128]{2,1,0:T(8,128)S(1)} %copy-done.1, f32[8192,128]{1,0:T(8,128)S(1)} %copy-done, f32[256,128]{1,0:T(8,128)S(1)} %pad_maximum_fusion.mix_ref), custom_call_target="tpu_custom_call" | custom-call | tf_op jit(solution)/shard_map/pallas_call | solution.py:227
  187.9 0.7 maximum_multiply_fusion
  (7 shorter events, 0.1 us)
Async XLA Ops:
  172.8 2.2 %copy-start = (f32[8192,128]{1,0:T(8,128)S(1)}, f32[8192,128]{1,0:T(8,128)}, u32[]{:S(2)}) copy-start(f32[8192,128]{1,0:T(8,128)} %matrix_ref.3) | copy-start | bytes 12582916
  175.0 3.4 %copy-start.1 = (f32[2,8192,128]{2,1,0:T(8,128)S(1)}, f32[2,8192,128]{2,1,0:T(8,128)}, u32[]{:S(2)}) copy-start(f32[2,8192,128]{2,1,0:T(8,128)} %get-tuple-element.7.panels_ref) | copy-start | bytes 25165828

commit v2 on v1

--- a/solution.py
+++ b/solution.py
@@ -11,7 +11,8 @@
 MESH = pl.DeviceIdType.MESH
 HIGHEST = lax.Precision.HIGHEST
 PANELS = 2
-LAG = 3
+LAG = 4
+BLOCK = 32
 
 
 def outer(a, b):
@@ -179,7 +180,7 @@
 
 def gather(matrix, n_row, n_x, n_z):
     rows, width = matrix.shape
-    tile = math.gcd(rows, 256)
+    tile = math.gcd(rows, 128)
     steps = rows // tile
     deep, wide = PANELS * width, (PANELS + 1) * width
     share = deep // n_row
@@ -213,62 +214,118 @@
     )(matrix)
 
 
-def update_kernel(panels_ref, matrix_ref, mix_ref, out_ref):
-    width = matrix_ref.shape[1]
-    keep = lax.axis_index("col") >= PANELS
-    product = jnp.dot(panels_ref[0], mix_ref[:width], precision=HIGHEST)
-    product += jnp.dot(panels_ref[1], mix_ref[width:], precision=HIGHEST)
-    out_ref[...] = jnp.where(keep, matrix_ref[...], 0.0) - product
-
-
-def update(panels, matrix, mix):
-    rows, width = matrix.shape
-    tile = math.gcd(rows, 1024)
-    return pl.pallas_call(
-        update_kernel,
-        grid=(rows // tile,),
-        out_shape=jax.ShapeDtypeStruct((rows, width), jnp.float32),
-        in_specs=[
-            pl.BlockSpec((PANELS, tile, width), lambda i: (0, i, 0)),
-            pl.BlockSpec((tile, width), lambda i: (i, 0)),
-            pl.BlockSpec((PANELS * width, width), lambda i: (0, 0)),
-        ],
-        out_specs=pl.BlockSpec((tile, width), lambda i: (i, 0)),
-        compiler_params=pltpu.CompilerParams(vmem_limit_bytes=40 * 1024 * 1024),
-    )(panels, matrix, mix)
-
-
-def product(a, b):
-    return jnp.dot(a, b, precision=HIGHEST)
-
-
-def inverse_of(lower_factor):
-    width = lower_factor.shape[0]
-    return jax.scipy.linalg.solve_triangular(
-        lower_factor, jnp.eye(width, dtype=jnp.float32), lower=True
+def product(a, b, over=((1,), (0,))):
+    return lax.dot_general(
+        a, b, (over, ((), ())), precision=HIGHEST, preferred_element_type=jnp.float32
     )
 
 
-def coefficients(sums, factor_scale, width):
-    col = lax.axis_index("col")
+def inverse_factor(gram):
+    width = gram.shape[0]
+    left, right = gram, eye(width)
+    row_id = lax.broadcasted_iota(jnp.int32, (BLOCK, 1), 0)
+    lane = lax.broadcasted_iota(jnp.int32, (BLOCK, width), 1)
+    done = []
+    for start in range(0, width, BLOCK):
+        p, e = left[:BLOCK], right[:BLOCK]
+        for s in range(BLOCK):
+            column = p[:, start + s:start + s + 1]
+            ratio = jnp.where(row_id > s, column / column[s:s + 1], 0.0)
+            p, e = p - ratio * p[s:s + 1], e - ratio * e[s:s + 1]
+        pivots = jnp.sum(jnp.where(lane == row_id + start, p, 0.0), axis=1, keepdims=True)
+        scale = 1.0 / jnp.sqrt(pivots)
+        p, e = p * scale, e * scale
+        done.append(e)
+        if start + BLOCK < width:
+            change = outer(p, jnp.concatenate([p, e], axis=1))
+            left = left[BLOCK:] - change[start + BLOCK:, :width]
+            right = right[BLOCK:] - change[start + BLOCK:, width:]
+    return jnp.concatenate(done, axis=0)
+
+
+def eye(width):
+    rows = lax.broadcasted_iota(jnp.int32, (width, width), 0)
+    return jnp.where(rows == lax.broadcasted_iota(jnp.int32, (width, width), 1), 1.0, 0.0)
+
+
+def coefficients(sums, factor_scale, width, col):
     g00, g01 = sums[:width, :width], sums[:width, width:2 * width]
-    g11 = sums[width:, width:2 * width]
+    g10, g11 = sums[width:, :width], sums[width:, width:2 * width]
     m0, m1 = sums[:width, 2 * width:], sums[width:, 2 * width:]
-    scaled_eye = factor_scale * jnp.eye(width, dtype=jnp.float32)
-    inv0 = inverse_of(jnp.linalg.cholesky(g00))
+    scaled_eye = factor_scale * eye(width)
+    down, turned = ((0,), (0,)), ((1,), (1,))
+    inv0 = inverse_factor(g00)
     both = product(inv0, jnp.concatenate([m0, g01], axis=1))
     cross0, r01 = both[:, :width], both[:, width:]
-    lower1 = jnp.linalg.cholesky(g11 - product(r01.T, r01))
-    inv1 = inverse_of(lower1)
-    scaled = factor_scale * product(jnp.concatenate([g00, g01.T], axis=0), inv0.T)
-    n0 = jnp.where(col == 0, scaled[:width], m0)
-    n1 = jnp.where(col == 0, scaled[width:], m1)
-    cross1 = product(inv1, n1 - product(r01.T, product(inv0, n0)))
+    inv1 = inverse_factor(g11 - product(r01, r01, down))
+    n0 = jnp.where(col == 0, factor_scale * product(g00, inv0, turned), m0)
+    n1 = jnp.where(col == 0, factor_scale * product(g10, inv0, turned), m1)
+    cross1 = product(inv1, n1 - product(r01, product(inv0, n0), down))
     t1 = jnp.where(col == 1, -scaled_eye, jnp.where(col == 0, 0.0, cross1))
     t0 = jnp.where(col == 0, -scaled_eye, jnp.where(col == 1, 0.0, cross0))
-    x1 = product(inv1.T, t1)
-    x0 = product(inv0.T, t0 - product(r01, x1))
-    return jnp.stack([cross0, cross1]) / factor_scale, jnp.concatenate([x0, x1], axis=0)
+    x1 = product(inv1, t1, down)
+    x0 = product(inv0, t0 - product(r01, x1), down)
+    return cross0, cross1, jnp.concatenate([x0, x1], axis=0)
+
+
+def halves(a):
+    high = a.astype(jnp.bfloat16)
+    return high, (a - high.astype(jnp.float32)).astype(jnp.bfloat16)
+
+
+def finish_kernel(
+    factor_scale, tile, panels_ref, matrix_ref, sums_ref, r_ref, out_ref,
+    panels, mine, result, load_sem, out_sem,
+):
+    rows, width = mine.shape
+    load_panels = pltpu.make_async_copy(panels_ref, panels, load_sem.at[0])
+    load_mine = pltpu.make_async_copy(matrix_ref, mine, load_sem.at[1])
+    load_panels.start()
+    load_mine.start()
+    col = lax.axis_index("col")
+    cross0, cross1, mix = coefficients(sums_ref[...], factor_scale, width, col)
+    r_ref[0] = cross0 / factor_scale
+    r_ref[1] = cross1 / factor_scale
+    mix_high, mix_low = halves(mix)
+    mix_both = jnp.concatenate([mix_high, mix_low], axis=1)
+    load_panels.wait()
+    load_mine.wait()
+    keep = col >= PANELS
+
+    @pl.loop(0, rows // tile)
+    def _(index):
+        at = pl.ds(pl.multiple_of(index * tile, tile), tile)
+        high, low = halves(jnp.concatenate([panels[0, at], panels[1, at]], axis=1))
+        main = jnp.dot(high, mix_both, preferred_element_type=jnp.float32)
+        rest = jnp.dot(low, mix_high, preferred_element_type=jnp.float32)
+        removed = main[:, :width] + (main[:, width:] + rest)
+        result[at] = jnp.where(keep, mine[at], 0.0) - removed
+        pltpu.make_async_copy(result.at[at], out_ref.at[at], out_sem).start()
+
+    pltpu.make_async_copy(result, out_ref, out_sem).wait()
+
+
+def finish(panels, matrix, sums, factor_scale):
+    rows, width = matrix.shape
+    anywhere = pl.BlockSpec(memory_space=pl.ANY)
+    in_vmem = pl.BlockSpec(memory_space=pltpu.VMEM)
+    return pl.pallas_call(
+        functools.partial(finish_kernel, factor_scale, math.gcd(rows, 512)),
+        out_shape=(
+            jax.ShapeDtypeStruct((PANELS, width, width), jnp.float32),
+            jax.ShapeDtypeStruct((rows, width), jnp.float32),
+        ),
+        in_specs=[anywhere, anywhere, in_vmem],
+        out_specs=(in_vmem, anywhere),
+        scratch_shapes=[
+            pltpu.VMEM((PANELS, rows, width), jnp.float32),
+            pltpu.VMEM((rows, width), jnp.float32),
+            pltpu.VMEM((rows, width), jnp.float32),
+            pltpu.SemaphoreType.DMA((2,)),
+            pltpu.SemaphoreType.DMA,
+        ],
+        compiler_params=pltpu.CompilerParams(vmem_limit_bytes=60 * 1024 * 1024),
+    )(panels, matrix, sums)
 
 
 def solution(mesh):
@@ -281,8 +338,7 @@
         rows, width = matrix.shape
         factor_scale = math.sqrt(rows * n_row)
         panels, sums = gather(matrix, n_row, n_x, n_z)
-        r_rows, mix = coefficients(sums, factor_scale, width)
-        return r_rows, update(panels, matrix, mix)
+        return finish(panels, matrix, sums, factor_scale)
 
     return jax.shard_map(
         local,

time: 189 us -> 148 us (0.78)
  other arithmetic: 46.5 us -> 0 us
  Pallas kernels: 129 us -> 148 us
  local copies, waits for them, and re-layouts: 7.8 us -> 0 us
  matrix products: 4.66 us -> 0 us
    another operation x10 -> x0, other arithmetic: 45.8 us -> none  [the longest x4 21 us: inverse_of(): jax.scipy.linalg.solve_triangular(lower_factor, jnp.eye(width, dtype=jnp....]
    pallas_call x1, Pallas kernels: 9.55 us -> 32 us  [finish(): pl.pallas_call(functools.partial(finish_kernel, factor_scale, math.gcd(ro...]
    unnamed x4 -> x0, local copies, waits for them, and re-layouts: 5.56 us -> none
    dot_general x9 -> x0, matrix products: 4.09 us -> none  [product(): return jnp.dot(a, b, precision=HIGHEST)]
    pallas_call x1, Pallas kernels: 119 us -> 116 us  [gather(): pl.pallas_call(functools.partial(gather_kernel, n_row, n_x, n_z, tile), o...]
where the time goes in v2:
time: 148 us
  Pallas kernels  148 us (100%)
    pallas_call x1, Pallas kernels, gather(): pl.pallas_call(functools.partial(gather_kernel, n_row, n_x, n_z, tile), o...  116 us
    pallas_call x1, Pallas kernels, finish(): pl.pallas_call(functools.partial(finish_kernel, factor_scale, math.gcd(ro...  32 us

profile of v2, /device:TPU:25, one launch (start us, length us, event | category | flops | bytes accessed | tf_op | source)
XLA Modules:
  0.0 148.3 jit_solution(16912468024376496841)
XLA Ops:
  0.6 115.7 %shard_map.30 = (f32[2,8192,128]{2,1,0:T(8,128)}, f32[256,384]{1,0:T(8,128)}) custom-call(f32[8192,128]{1,0:T(8,128)} %matrix_ref.3), custom_call_target="tpu_custom_call" | custom-call | tf_op jit(solution)/shard_map/pallas_call | solution.py:188
  116.3 32.0 %shard_map.31 = (f32[2,128,128]{2,1,0:T(8,128)}, f32[8192,128]{1,0:T(8,128)}) custom-call(f32[2,8192,128]{2,1,0:T(8,128)} %get-tuple-element.4.panels_ref, f32[8192,128]{1,0:T(8,128)} %matrix_ref.3, f32[256,384]{1,0:T(8,128)} %get-tuple-element.5.sums_ref), custom_call_target="tpu_custom_call" | custom-call | tf_op jit(solution)/shard_map/pallas_call | solution.py:312

commit v3 on v2

v3 whole, which is shorter than its diff:
```python
import functools
import math

import jax
import jax.numpy as jnp
from jax import lax
from jax.experimental import pallas as pl
from jax.experimental.pallas import tpu as pltpu
from jax.sharding import PartitionSpec as P

MESH = pl.DeviceIdType.MESH
HIGHEST = lax.Precision.HIGHEST
PANELS = 2
LAG = 4
BLOCK = 32
EXTRA = 2
AHEAD = 6


def outer(a, b):
    return lax.dot_general(
        a, b, (((0,), (0,)), ((), ())), precision=HIGHEST, preferred_element_type=jnp.float32
    )


def gather_kernel(
    n_row, n_x, n_z, tile,
    matrix_ref, panels_out, sums_out,
    panels, mine, mixed, half, theirs, parts, total,
    mine_sem, recv_sem, send_sem, out_sem, scatter_send, scatter_recv, back_send, back_recv,
    swap_sem,
):
    rows, width = mine.shape
    steps = rows // tile
    row = lax.axis_index("row")
    col = lax.axis_index("col")
    x = lax.rem(col, n_x)
    z = col // n_x

    barrier = pltpu.get_barrier_semaphore()
    neighbours = (
        (x > 0, col - 1), (x < n_x - 1, col + 1), (z > 0, col - n_x), (z < n_z - 1, col + n_x)
    )
    for there, other in neighbours:
        @pl.when(there)
        def _():
            pl.semaphore_signal(barrier, inc=1, device_id={"col": other}, device_id_type=MESH)
    for step in range(1, n_row):
        peer = lax.rem(row + step, n_row)
        pl.semaphore_signal(barrier, inc=1, device_id={"row": peer}, device_id_type=MESH)
    load_mine = pltpu.make_async_copy(matrix_ref, mine, mine_sem)
    load_mine.start()
    mixed[...] = jnp.zeros_like(mixed)
    peers = n_row - 1
    for there, _ in neighbours:
        peers += jnp.where(there, 1, 0)
    pl.semaphore_wait(barrier, peers)

    def span(panel, index):
        turned = jnp.logical_and(panel == 1, index < steps)
        place = jnp.where(turned, steps - 1 - index, index)
        return pl.ds(pl.multiple_of(place * tile, tile), tile)

    def children(panel):
        return (
            (jnp.logical_and(x == panel, z < n_z - 1), col + n_x),
            (jnp.logical_and(x >= panel, x < n_x - 1), col + 1),
            (jnp.logical_and(x <= panel, x > 0), col - 1),
        )

    def forward(panel, index, source, which=(0, 1, 2)):
        for child, (there, other) in enumerate(children(panel)):
            if child not in which:
                continue

            @pl.when(there)
            def _():
                pltpu.make_async_remote_copy(
                    src_ref=source.at[span(panel, index)],
                    dst_ref=panels.at[panel, span(panel, index)],
                    send_sem=send_sem.at[panel, child],
                    recv_sem=recv_sem.at[panel, index],
                    device_id={"col": other},
                    device_id_type=MESH,
                ).start()

    def keep(panel, index):
        pltpu.make_async_copy(
            panels.at[panel, span(panel, index)],
            panels_out.at[panel, span(panel, index)],
            out_sem.at[panel],
        ).start()

    def take(panel, index):
        here = panels.at[panel, span(panel, index)]
        pltpu.make_async_copy(here, here, recv_sem.at[panel, index]).wait()
        forward(panel, index, panels.at[panel])
        keep(panel, index)

    def add(panel, index, source):
        at = span(panel, index)
        block = pl.ds(pl.multiple_of(panel * width, width), width)
        mixed[block] += outer(source[at], mine[at])

    share = mixed.shape[0] // n_row

    def part(index):
        return pl.ds(pl.multiple_of(index * share, share), share)

    def sum_over_row(source, turn):
        copies = []
        for step in range(1, n_row):
            peer = lax.rem(row + step, n_row)
            copies.append(pltpu.make_async_remote_copy(
                src_ref=source.at[part(peer)],
                dst_ref=parts.at[turn, step - 1],
                send_sem=scatter_send.at[turn, step - 1],
                recv_sem=scatter_recv.at[turn, step - 1],
                device_id={"row": peer},
                device_id_type=MESH,
            ))
            copies[-1].start()
        summed = source[part(row)]
        for step, copy in enumerate(copies):
            copy.wait_recv()
            summed += parts[turn, step]
        result = total.at[turn]
        result[part(row)] = summed
        backs = []
        for step in range(1, n_row):
            peer = lax.rem(row + step, n_row)
            backs.append(pltpu.make_async_remote_copy(
                src_ref=result.at[part(row)],
                dst_ref=result.at[part(row)],
                send_sem=back_send.at[turn, step - 1],
                recv_sem=back_recv.at[turn, step - 1],
                device_id={"row": peer},
                device_id_type=MESH,
            ))
            backs[-1].start()
        for copy in backs:
            copy.wait_recv()
        for copy in copies + backs:
            copy.wait_send()

    main = jnp.where(x == 1, 1, 0)
    second = 1 - main
    owner = col < PANELS
    middle = steps // 2
    load_mine.wait()

    @pl.when(owner)
    def _():
        @pl.loop(0, middle + AHEAD)
        def _(index):
            forward(col, index, matrix_ref)

        @pl.loop(middle + AHEAD, steps)
        def _(index):
            forward(col, index, matrix_ref, (0,))

        own = pltpu.make_async_copy(
            mine, panels_out.at[col, pl.ds(0, rows)], out_sem.at[col]
        )
        own.start()

        @pl.loop(0, steps)
        def _(index):
            add(col, index, mine)

        @pl.loop(0, middle)
        def _(index):
            take(second, index)
            add(second, index, panels.at[second])

        half[...] = mixed[...]
        sum_over_row(half, 0)
        swap = pltpu.make_async_remote_copy(
            src_ref=total.at[0],
            dst_ref=theirs,
            send_sem=swap_sem.at[0],
            recv_sem=swap_sem.at[1],
            device_id={"col": 1 - col},
            device_id_type=MESH,
        )
        swap.start()

        @pl.loop(middle + AHEAD, steps)
        def _(index):
            forward(col, index, matrix_ref, (1, 2))

        swap.wait()
        first = col == 0
        ours, other = total[0], theirs[...]
        left = jnp.where(first, ours, other)
        right = jnp.where(first, other, ours)
        inv0 = inverse_factor(left[:width])
        r01 = product(inv0, right[:width]) + product(inv0, left[width:], ((1,), (1,)))
        inv1 = inverse_factor(right[width:] - product(r01, r01, ((0,), (0,))))
        extra = pl.ds(rows, width)
        panels[col, extra] = jnp.where(first, inv0, inv1)
        panels[col, pl.ds(rows + width, width)] = r01
        for index in range(steps, steps + EXTRA):
            forward(col, index, panels.at[col])
            keep(col, index)

        @pl.loop(middle, steps)
        def _(index):
            take(second, index)
            add(second, index, panels.at[second])

        for index in range(steps, steps + EXTRA):
            take(second, index)

    @pl.when(jnp.logical_not(owner))
    def _():
        @pl.loop(0, steps + EXTRA + LAG)
        def _(step):
            @pl.when(step < steps + EXTRA)
            def _():
                take(main, step)

            @pl.when(step >= LAG)
            def _():
                take(second, step - LAG)

            @pl.when(step < steps)
            def _():
                add(main, step, panels.at[main])

            @pl.when(jnp.logical_and(step >= LAG, step < steps + LAG))
            def _():
                add(second, step - LAG, panels.at[second])

    sum_over_row(mixed, 1)
    sums_out[...] = total[1]

    for panel in range(PANELS):
        pltpu.make_async_copy(panels.at[panel], panels_out.at[panel], out_sem.at[panel]).wait()
        for child, (there, other) in enumerate(children(panel)):
            @pl.when(there)
            def _():
                pltpu.make_async_remote_copy(
                    src_ref=panels.at[panel],
                    dst_ref=panels.at[panel],
                    send_sem=send_sem.at[panel, child],
                    recv_sem=recv_sem.at[panel, 0],
                    device_id={"col": other},
                    device_id_type=MESH,
                ).wait_send()


def gather(matrix, n_row, n_x, n_z):
    rows, width = matrix.shape
    tile = width
    steps = rows // tile
    assert rows % (2 * tile) == 0
    deep, tall = PANELS * width, rows + EXTRA * width
    share = deep // n_row
    anywhere = pl.BlockSpec(memory_space=pl.ANY)
    return pl.pallas_call(
        functools.partial(gather_kernel, n_row, n_x, n_z, tile),
        out_shape=(
            jax.ShapeDtypeStruct((PANELS, tall, width), jnp.float32),
            jax.ShapeDtypeStruct((deep, width), jnp.float32),
        ),
        in_specs=[anywhere],
        out_specs=(anywhere, pl.BlockSpec(memory_space=pltpu.VMEM)),
        scratch_shapes=[
            pltpu.VMEM((PANELS, tall, width), jnp.float32),
            pltpu.VMEM((rows, width), jnp.float32),
            pltpu.VMEM((deep, width), jnp.float32),
            pltpu.VMEM((deep, width), jnp.float32),
            pltpu.VMEM((deep, width), jnp.float32),
            pltpu.VMEM((2, n_row - 1, share, width), jnp.float32),
            pltpu.VMEM((2, deep, width), jnp.float32),
            pltpu.SemaphoreType.DMA,
            pltpu.SemaphoreType.DMA((PANELS, steps + EXTRA)),
            pltpu.SemaphoreType.DMA((PANELS, 3)),
            pltpu.SemaphoreType.DMA((PANELS,)),
            pltpu.SemaphoreType.DMA((2, n_row - 1)),
            pltpu.SemaphoreType.DMA((2, n_row - 1)),
            pltpu.SemaphoreType.DMA((2, n_row - 1)),
            pltpu.SemaphoreType.DMA((2, n_row - 1)),
            pltpu.SemaphoreType.DMA((2,)),
        ],
        compiler_params=pltpu.CompilerParams(
            collective_id=0, has_side_effects=True, vmem_limit_bytes=60 * 1024 * 1024
        ),
    )(matrix)


def product(a, b, over=((1,), (0,))):
    return lax.dot_general(
        a, b, (over, ((), ())), precision=HIGHEST, preferred_element_type=jnp.float32
    )


def inverse_factor(gram):
    width = gram.shape[0]
    left, right = gram, eye(width)
    row_id = lax.broadcasted_iota(jnp.int32, (BLOCK, 1), 0)
    lane = lax.broadcasted_iota(jnp.int32, (BLOCK, width), 1)
    done = []
    for start in range(0, width, BLOCK):
        p, e = left[:BLOCK], right[:BLOCK]
        for s in range(BLOCK):
            column = p[:, start + s:start + s + 1]
            ratio = jnp.where(row_id > s, column / column[s:s + 1], 0.0)
            p, e = p - ratio * p[s:s + 1], e - ratio * e[s:s + 1]
        pivots = jnp.sum(jnp.where(lane == row_id + start, p, 0.0), axis=1, keepdims=True)
        scale = 1.0 / jnp.sqrt(pivots)
        p, e = p * scale, e * scale
        done.append(e)
        if start + BLOCK < width:
            change = outer(p, jnp.concatenate([p, e], axis=1))
            left = left[BLOCK:] - change[start + BLOCK:, :width]
            right = right[BLOCK:] - change[start + BLOCK:, width:]
    return jnp.concatenate(done, axis=0)


def eye(width):
    rows = lax.broadcasted_iota(jnp.int32, (width, width), 0)
    return jnp.where(rows == lax.broadcasted_iota(jnp.int32, (width, width), 1), 1.0, 0.0)


def coefficients(sums, inv0, r01, inv1, factor_scale, width, col):
    m0, m1 = sums[:width], sums[width:]
    scaled_eye = factor_scale * eye(width)
    down, turned = ((0,), (0,)), ((1,), (1,))
    cross0 = product(inv0, m0)
    n0 = jnp.where(col == 0, factor_scale * product(m0, inv0, turned), m0)
    n1 = jnp.where(col == 0, factor_scale * product(m1, inv0, turned), m1)
    cross1 = product(inv1, n1 - product(r01, product(inv0, n0), down))
    t1 = jnp.where(col == 1, -scaled_eye, jnp.where(col == 0, 0.0, cross1))
    t0 = jnp.where(col == 0, -scaled_eye, jnp.where(col == 1, 0.0, cross0))
    x1 = product(inv1, t1, down)
    x0 = product(inv0, t0 - product(r01, x1), down)
    return cross0, cross1, jnp.concatenate([x0, x1], axis=0)


def halves(a):
    high = a.astype(jnp.bfloat16)
    return high, (a - high.astype(jnp.float32)).astype(jnp.bfloat16)


def finish_kernel(
    factor_scale, tile, panels_ref, matrix_ref, sums_ref, r_ref, out_ref,
    panels, mine, factors, result, load_sem, out_sem,
):
    rows, width = mine.shape
    load_factors = pltpu.make_async_copy(
        panels_ref.at[:, pl.ds(rows, EXTRA * width)], factors, load_sem.at[2]
    )
    load_panels = pltpu.make_async_copy(
        panels_ref.at[:, pl.ds(0, rows)], panels, load_sem.at[0]
    )
    load_mine = pltpu.make_async_copy(matrix_ref, mine, load_sem.at[1])
    load_factors.start()
    load_panels.start()
    load_mine.start()
    col = lax.axis_index("col")
    load_factors.wait()
    inv0, r01, inv1 = factors[0, :width], factors[0, width:], factors[1, :width]
    cross0, cross1, mix = coefficients(
        sums_ref[...], inv0, r01, inv1, factor_scale, width, col
    )
    r_ref[0] = cross0 / factor_scale
    r_ref[1] = cross1 / factor_scale
    mix_high, mix_low = halves(mix)
    mix_both = jnp.concatenate([mix_high, mix_low], axis=1)
    load_panels.wait()
    load_mine.wait()
    keep = col >= PANELS

    @pl.loop(0, rows // tile)
    def _(index):
        at = pl.ds(pl.multiple_of(index * tile, tile), tile)
        high, low = halves(jnp.concatenate([panels[0, at], panels[1, at]], axis=1))
        main = jnp.dot(high, mix_both, preferred_element_type=jnp.float32)
        rest = jnp.dot(low, mix_high, preferred_element_type=jnp.float32)
        removed = main[:, :width] + (main[:, width:] + rest)
        result[at] = jnp.where(keep, mine[at], 0.0) - removed
        pltpu.make_async_copy(result.at[at], out_ref.at[at], out_sem).start()

    pltpu.make_async_copy(result, out_ref, out_sem).wait()


def finish(panels, matrix, sums, factor_scale):
    rows, width = matrix.shape
    anywhere = pl.BlockSpec(memory_space=pl.ANY)
    in_vmem = pl.BlockSpec(memory_space=pltpu.VMEM)
    return pl.pallas_call(
        functools.partial(finish_kernel, factor_scale, math.gcd(rows, 512)),
        out_shape=(
            jax.ShapeDtypeStruct((PANELS, width, width), jnp.float32),
            jax.ShapeDtypeStruct((rows, width), jnp.float32),
        ),
        in_specs=[anywhere, anywhere, in_vmem],
        out_specs=(in_vmem, anywhere),
        scratch_shapes=[
            pltpu.VMEM((PANELS, rows, width), jnp.float32),
            pltpu.VMEM((rows, width), jnp.float32),
            pltpu.VMEM((PANELS, EXTRA * width, width), jnp.float32),
            pltpu.VMEM((rows, width), jnp.float32),
            pltpu.SemaphoreType.DMA((3,)),
            pltpu.SemaphoreType.DMA,
        ],
        compiler_params=pltpu.CompilerParams(vmem_limit_bytes=60 * 1024 * 1024),
    )(panels, matrix, sums)


def solution(mesh):
    n_row, n_col = mesh.shape["row"], mesh.shape["col"]
    n_x = max(PANELS, n_row // 2)
    n_z = n_col // n_x
    assert n_x * n_z == n_col

    def local(matrix):
        rows, width = matrix.shape
        factor_scale = math.sqrt(rows * n_row)
        panels, sums = gather(matrix, n_row, n_x, n_z)
        return finish(panels, matrix, sums, factor_scale)

    return jax.shard_map(
        local,
        mesh=mesh,
        in_specs=(P("row", "col"),),
        out_specs=(P(None, None, "col"), P("row", "col")),
        check_vma=False,
    )
```

time: 148 us -> 127 us (0.86)
  Pallas kernels: 148 us -> 126 us
    pallas_call x1, Pallas kernels: 32 us -> 11.9 us  [finish(): pl.pallas_call(functools.partial(finish_kernel, factor_scale, math.gcd(ro...]
where the time goes in v3:
time: 127 us
  Pallas kernels  126 us (99%)
    pallas_call x1, Pallas kernels, gather(): pl.pallas_call(functools.partial(gather_kernel, n_row, n_x, n_z, tile), o...  114 us
    pallas_call x1, Pallas kernels, finish(): pl.pallas_call(functools.partial(finish_kernel, factor_scale, math.gcd(ro...  11.9 us

profile of v3, /device:TPU:25, one launch (start us, length us, event | category | flops | bytes accessed | tf_op | source)
XLA Modules:
  0.0 127.1 jit_solution(16527683101650528684)
XLA Ops:
  0.6 114.5 %shard_map.30 = (f32[2,8448,128]{2,1,0:T(8,128)}, f32[256,128]{1,0:T(8,128)}) custom-call(f32[8192,128]{1,0:T(8,128)} %matrix_ref.3), custom_call_target="tpu_custom_call" | custom-call | tf_op jit(solution)/shard_map/pallas_call | solution.py:261
  115.1 11.9 %shard_map.31 = (f32[2,128,128]{2,1,0:T(8,128)}, f32[8192,128]{1,0:T(8,128)}) custom-call(f32[2,8448,128]{2,1,0:T(8,128)} %get-tuple-element.4.panels_ref, f32[8192,128]{1,0:T(8,128)} %matrix_ref.3, f32[256,128]{1,0:T(8,128)} %get-tuple-element.5.sums_ref), custom_call_target="tpu_custom_call" | custom-call | tf_op jit(solution)/shard_map/pallas_call | solution.py:393

commit v4 on v3

--- a/solution.py
+++ b/solution.py
@@ -147,7 +147,6 @@
     second = 1 - main
     owner = col < PANELS
     middle = steps // 2
-    load_mine.wait()
 
     @pl.when(owner)
     def _():
@@ -159,6 +158,7 @@
         def _(index):
             forward(col, index, matrix_ref, (0,))
 
+        load_mine.wait()
         own = pltpu.make_async_copy(
             mine, panels_out.at[col, pl.ds(0, rows)], out_sem.at[col]
         )
@@ -199,7 +199,8 @@
         inv1 = inverse_factor(right[width:] - product(r01, r01, ((0,), (0,))))
         extra = pl.ds(rows, width)
         panels[col, extra] = jnp.where(first, inv0, inv1)
-        panels[col, pl.ds(rows + width, width)] = r01
+        corner = -product(product(inv1, r01, ((1,), (1,))), inv0)
+        panels[col, pl.ds(rows + width, width)] = corner
         for index in range(steps, steps + EXTRA):
             forward(col, index, panels.at[col])
             keep(col, index)
@@ -209,12 +210,11 @@
             take(second, index)
             add(second, index, panels.at[second])
 
-        for index in range(steps, steps + EXTRA):
-            take(second, index)
-
     @pl.when(jnp.logical_not(owner))
     def _():
-        @pl.loop(0, steps + EXTRA + LAG)
+        load_mine.wait()
+
+        @pl.loop(0, steps + LAG)
         def _(step):
             @pl.when(step < steps + EXTRA)
             def _():
@@ -228,12 +228,14 @@
             def _():
                 add(main, step, panels.at[main])
 
-            @pl.when(jnp.logical_and(step >= LAG, step < steps + LAG))
+            @pl.when(step >= LAG)
             def _():
                 add(second, step - LAG, panels.at[second])
 
     sum_over_row(mixed, 1)
     sums_out[...] = total[1]
+    for index in range(steps, steps + EXTRA):
+        take(second, index)
 
     for panel in range(PANELS):
         pltpu.make_async_copy(panels.at[panel], panels_out.at[panel], out_sem.at[panel]).wait()
@@ -324,18 +326,16 @@
     return jnp.where(rows == lax.broadcasted_iota(jnp.int32, (width, width), 1), 1.0, 0.0)
 
 
-def coefficients(sums, inv0, r01, inv1, factor_scale, width, col):
-    m0, m1 = sums[:width], sums[width:]
+def coefficients(sums, inv0, corner, inv1, factor_scale, width, col):
     scaled_eye = factor_scale * eye(width)
     down, turned = ((0,), (0,)), ((1,), (1,))
-    cross0 = product(inv0, m0)
-    n0 = jnp.where(col == 0, factor_scale * product(m0, inv0, turned), m0)
-    n1 = jnp.where(col == 0, factor_scale * product(m1, inv0, turned), m1)
-    cross1 = product(inv1, n1 - product(r01, product(inv0, n0), down))
+    cross0 = product(inv0, sums[:width])
+    seen = jnp.where(col == 0, factor_scale * product(sums, inv0, turned), sums)
+    cross1 = product(jnp.concatenate([corner, inv1], axis=1), seen)
     t1 = jnp.where(col == 1, -scaled_eye, jnp.where(col == 0, 0.0, cross1))
     t0 = jnp.where(col == 0, -scaled_eye, jnp.where(col == 1, 0.0, cross0))
     x1 = product(inv1, t1, down)
-    x0 = product(inv0, t0 - product(r01, x1), down)
+    x0 = product(inv0, t0, down) + product(corner, t1, down)
     return cross0, cross1, jnp.concatenate([x0, x1], axis=0)
 
 
@@ -349,32 +349,40 @@
     panels, mine, factors, result, load_sem, out_sem,
 ):
     rows, width = mine.shape
+    pieces = rows // tile
     load_factors = pltpu.make_async_copy(
-        panels_ref.at[:, pl.ds(rows, EXTRA * width)], factors, load_sem.at[2]
-    )
-    load_panels = pltpu.make_async_copy(
-        panels_ref.at[:, pl.ds(0, rows)], panels, load_sem.at[0]
-    )
-    load_mine = pltpu.make_async_copy(matrix_ref, mine, load_sem.at[1])
+        panels_ref.at[:, pl.ds(rows, EXTRA * width)], factors, load_sem.at[2, 0]
+    )
     load_factors.start()
-    load_panels.start()
-    load_mine.start()
+
+    def loads(index):
+        at = pl.ds(pl.multiple_of(index * tile, tile), tile)
+        return (
+            pltpu.make_async_copy(panels_ref.at[:, at], panels.at[:, at], load_sem.at[0, index]),
+            pltpu.make_async_copy(matrix_ref.at[at], mine.at[at], load_sem.at[1, index]),
+        )
+
+    @pl.loop(0, pieces)
+    def _(index):
+        for load in loads(index):
+            load.start()
+
     col = lax.axis_index("col")
     load_factors.wait()
-    inv0, r01, inv1 = factors[0, :width], factors[0, width:], factors[1, :width]
+    inv0, corner, inv1 = factors[0, :width], factors[0, width:], factors[1, :width]
     cross0, cross1, mix = coefficients(
-        sums_ref[...], inv0, r01, inv1, factor_scale, width, col
+        sums_ref[...], inv0, corner, inv1, factor_scale, width, col
     )
     r_ref[0] = cross0 / factor_scale
     r_ref[1] = cross1 / factor_scale
     mix_high, mix_low = halves(mix)
     mix_both = jnp.concatenate([mix_high, mix_low], axis=1)
-    load_panels.wait()
-    load_mine.wait()
     keep = col >= PANELS
 
-    @pl.loop(0, rows // tile)
+    @pl.loop(0, pieces)
     def _(index):
+        for load in loads(index):
+            load.wait()
         at = pl.ds(pl.multiple_of(index * tile, tile), tile)
         high, low = halves(jnp.concatenate([panels[0, at], panels[1, at]], axis=1))
         main = jnp.dot(high, mix_both, preferred_element_type=jnp.float32)
@@ -388,10 +396,11 @@
 
 def finish(panels, matrix, sums, factor_scale):
     rows, width = matrix.shape
+    tile = math.gcd(rows, 1024)
     anywhere = pl.BlockSpec(memory_space=pl.ANY)
     in_vmem = pl.BlockSpec(memory_space=pltpu.VMEM)
     return pl.pallas_call(
-        functools.partial(finish_kernel, factor_scale, math.gcd(rows, 512)),
+        functools.partial(finish_kernel, factor_scale, tile),
         out_shape=(
             jax.ShapeDtypeStruct((PANELS, width, width), jnp.float32),
             jax.ShapeDtypeStruct((rows, width), jnp.float32),
@@ -403,7 +412,7 @@
             pltpu.VMEM((rows, width), jnp.float32),
             pltpu.VMEM((PANELS, EXTRA * width, width), jnp.float32),
             pltpu.VMEM((rows, width), jnp.float32),
-            pltpu.SemaphoreType.DMA((3,)),
+            pltpu.SemaphoreType.DMA((3, rows // tile)),
             pltpu.SemaphoreType.DMA,
         ],
         compiler_params=pltpu.CompilerParams(vmem_limit_bytes=60 * 1024 * 1024),

time: 127 us -> 123 us (0.969)
  Pallas kernels: 126 us -> 122 us
    pallas_call x1, Pallas kernels: 11.9 us -> 8.6 us  [finish(): pl.pallas_call(functools.partial(finish_kernel, factor_scale, tile), out_...]
where the time goes in v4:
time: 123 us
  Pallas kernels  122 us (99%)
    pallas_call x1, Pallas kernels, gather(): pl.pallas_call(functools.partial(gather_kernel, n_row, n_x, n_z, tile), o...  113 us
    pallas_call x1, Pallas kernels, finish(): pl.pallas_call(functools.partial(finish_kernel, factor_scale, tile), out_...  8.6 us

profile of v4, /device:TPU:25, one launch (start us, length us, event | category | flops | bytes accessed | tf_op | source)
XLA Modules:
  0.0 122.7 jit_solution(6608911897283098623)
XLA Ops:
  0.6 113.4 %shard_map.30 = (f32[2,8448,128]{2,1,0:T(8,128)}, f32[256,128]{1,0:T(8,128)}) custom-call(f32[8192,128]{1,0:T(8,128)} %matrix_ref.3), custom_call_target="tpu_custom_call" | custom-call | tf_op jit(solution)/shard_map/pallas_call | solution.py:263
  114.1 8.6 %shard_map.31 = (f32[2,128,128]{2,1,0:T(8,128)}, f32[8192,128]{1,0:T(8,128)}) custom-call(f32[2,8448,128]{2,1,0:T(8,128)} %get-tuple-element.4.panels_ref, f32[8192,128]{1,0:T(8,128)} %matrix_ref.3, f32[256,128]{1,0:T(8,128)} %get-tuple-element.5.sums_ref), custom_call_target="tpu_custom_call" | custom-call | tf_op jit(solution)/shard_map/pallas_call | solution.py:402

commit v5 on v4

--- a/solution.py
+++ b/solution.py
@@ -396,7 +396,7 @@
 
 def finish(panels, matrix, sums, factor_scale):
     rows, width = matrix.shape
-    tile = math.gcd(rows, 1024)
+    tile = math.gcd(rows, 512)
     anywhere = pl.BlockSpec(memory_space=pl.ANY)
     in_vmem = pl.BlockSpec(memory_space=pltpu.VMEM)
     return pl.pallas_call(

time: 123 us -> 124 us (level)
  no operation moved by 1% of the time
where the time goes in v5:
time: 124 us
  Pallas kernels  123 us (99%)
    pallas_call x1, Pallas kernels, gather(): pl.pallas_call(functools.partial(gather_kernel, n_row, n_x, n_z, tile), o...  113 us
    pallas_call x1, Pallas kernels, finish(): pl.pallas_call(functools.partial(finish_kernel, factor_scale, tile), out_...  9.72 us

profile of v5, /device:TPU:25, one launch (start us, length us, event | category | flops | bytes accessed | tf_op | source)
XLA Modules:
  0.0 123.8 jit_solution(8579346039437737542)
XLA Ops:
  0.6 113.4 %shard_map.30 = (f32[2,8448,128]{2,1,0:T(8,128)}, f32[256,128]{1,0:T(8,128)}) custom-call(f32[8192,128]{1,0:T(8,128)} %matrix_ref.3), custom_call_target="tpu_custom_call" | custom-call | tf_op jit(solution)/shard_map/pallas_call | solution.py:263
  114.1 9.7 %shard_map.31 = (f32[2,128,128]{2,1,0:T(8,128)}, f32[8192,128]{1,0:T(8,128)}) custom-call(f32[2,8448,128]{2,1,0:T(8,128)} %get-tuple-element.4.panels_ref, f32[8192,128]{1,0:T(8,128)} %matrix_ref.3, f32[256,128]{1,0:T(8,128)} %get-tuple-element.5.sums_ref), custom_call_target="tpu_custom_call" | custom-call | tf_op jit(solution)/shard_map/pallas_call | solution.py:402
